TPU v7x, 128 devices: a whole 4x4x4 slice. The times are simulated.
128 devices in a mesh: px: 8 (over x, core), py: 16 (over y, z).
Axes of the slice: x: 4, y: 4, z: 4, core: 2. Of those that a mesh axis runs over, the one named last changes fastest.
Arguments:
- cell_ids: int32 [131072, 128], P(('px', 'py')), may hold values from 0 to 32767
- masses: bfloat16 [131072, 128], P(('px', 'py')), may hold values from 0.5 to 2
- block_dest: int32 [131072, 1], P(('px', 'py')), may hold values from 0 to 1023; in each aligned block of 1024 rows (0 to 1023, 1024 to 2047, ...) at most 2 rows name the same one
- block_count: int32 [131072], P(('px', 'py')), may hold values from 1 to 128
- screen: float32 [8], replicated, may hold values from 0.02 to 0.2
Outputs:
- potential_modes: float32 [8, 128, 256], P(None, None, ('px', 'py'))
Inputs may be any that keep to these rules, and one draw needn't show every extreme that they name: `block_dest`: tile t lies on device t // 8 (devices numbered px-major) and plane t % 8. Among the 1024 blocks of one device no tile is named more than 2 times, a bound that some block reaches. `block_count`: the live particles of a block are its first ones. `cell_ids`: A cell c is row c // 128 and column c % (128) of the tile.
All inputs are finite; a program needn't handle non-finite values.
Results may differ from a plain program's by a relative error of at most 0.0003.
Values may be sent and summed in bfloat16 or wider, within the bound.
A program may use at most 64 MiB of HBM per device.

v0:
```python
import math
import jax
import jax.numpy as jnp
from jax import lax
from jax.sharding import PartitionSpec as P

NY = 2048
NZ = 2048
KY = 128
KZ = 128
CAP = 2
HIGHEST_PREC = lax.Precision.HIGHEST


def column_table(col_count):
    col_index = lax.broadcasted_iota(jnp.int32, (col_count, 2 * KZ), 0)
    col_slot = lax.broadcasted_iota(jnp.int32, (col_count, 2 * KZ), 1)
    col_freq = col_slot // 2 - KZ // 2
    col_phase = 2.0 * math.pi / NZ * jnp.remainder(col_freq * col_index, NZ).astype(jnp.float32)
    return jnp.where(col_slot % 2 == 0, jnp.cos(col_phase), -jnp.sin(col_phase))


def row_transform(row_coord, columns):
    y_freq = lax.broadcasted_iota(jnp.int32, row_coord.shape, 0) - KY // 2
    yphase = 2.0 * math.pi / NY * jnp.remainder(y_freq * row_coord, NY).astype(jnp.float32)
    cos_part = jnp.einsum("kp,lpc->lkc", jnp.cos(yphase), columns, precision=HIGHEST_PREC)
    sin_part = jnp.einsum("kp,lpc->lkc", jnp.sin(yphase), columns, precision=HIGHEST_PREC)
    real_part = cos_part[:, :, 0::2] + sin_part[:, :, 1::2]
    imag_part = cos_part[:, :, 1::2] - sin_part[:, :, 0::2]
    return jnp.stack([real_part, imag_part], axis=-1).reshape(
        columns.shape[0], row_coord.shape[0], columns.shape[2]
    )


def shards(cell_ids, masses, block_dest, block_count, screen):
    size_x = lax.axis_size("px")
    size_y = lax.axis_size("py")
    devices = size_x * size_y
    num_planes = screen.shape[0]
    blocks = cell_ids.shape[0]
    block_size = cell_ids.shape[1]
    tile_rows = NY // size_x
    tile_cols = NZ // size_y
    row_share = tile_rows // size_y
    col_share = 2 * KZ // devices
    num_tiles = devices * num_planes
    dest_tile = block_dest[:, 0]
    places = lax.broadcasted_iota(jnp.int32, (blocks, block_size), 1)
    weight = jnp.where(places < block_count[:, None], masses, jnp.zeros_like(masses))
    order_row = lax.broadcasted_iota(jnp.int32, (blocks, blocks), 0)
    order_col = lax.broadcasted_iota(jnp.int32, (blocks, blocks), 1)
    before = (dest_tile[:, None] == dest_tile[None, :]) & (order_col < order_row)
    slot_rank = jnp.sum(before.astype(jnp.int32), axis=1)
    owner_dev = dest_tile // num_planes
    plane_of = dest_tile % num_planes
    slot_index = (plane_of * devices + owner_dev) * CAP + slot_rank
    send_cells = jnp.zeros((num_tiles * CAP, block_size), jnp.int32).at[slot_index].set(cell_ids)
    send_mass = jnp.zeros((num_tiles * CAP, block_size), jnp.bfloat16).at[slot_index].set(weight)
    num_slots = devices * CAP * block_size
    send_cells = send_cells.reshape(num_planes, devices, CAP, block_size)
    send_mass = send_mass.reshape(num_planes, devices, CAP, block_size)
    recv_cells, recv_mass = (
        lax.all_to_all(send_cells, ("px", "py"), split_axis=1, concat_axis=1, tiled=True),
        lax.all_to_all(send_mass, ("px", "py"), split_axis=1, concat_axis=1, tiled=True),
    )
    plane_cells = recv_cells.reshape(num_planes, num_slots)
    plane_mass = recv_mass.reshape(num_planes, num_slots)

    def deposit(packed):
        cell_row, mass_row = packed
        row_of = cell_row // tile_cols
        col_of = cell_row % tile_cols
        row_iota = lax.broadcasted_iota(jnp.int32, (num_slots, tile_rows), 1)
        col_iota = lax.broadcasted_iota(jnp.int32, (num_slots, tile_cols), 1)
        onehot_rows = (row_iota == row_of[:, None]).astype(jnp.bfloat16)
        mass_cols = jnp.where(
            col_iota == col_of[:, None], mass_row[:, None], jnp.zeros((), jnp.bfloat16)
        )
        return lax.dot_general(
            onehot_rows, mass_cols, (((0,), (0,)), ((), ())), preferred_element_type=jnp.float32
        )

    density = lax.map(deposit, (plane_cells, plane_mass))
    z_slab = lax.all_to_all(density, "py", split_axis=1, concat_axis=2, tiled=True)
    ztable = column_table(NZ)
    spectra = jnp.dot(
        z_slab.reshape(num_planes * row_share, NZ),
        ztable,
        precision=HIGHEST_PREC,
        preferred_element_type=jnp.float32,
    )
    spectra = spectra.reshape(num_planes, row_share, 2 * KZ)
    positions = lax.broadcasted_iota(jnp.int32, (KY, NY), 1)
    columns = lax.all_to_all(spectra, ("px", "py"), split_axis=2, concat_axis=1, tiled=True)
    mode_values = row_transform(positions, columns)
    device = lax.axis_index("px") * size_y + lax.axis_index("py")
    z_mode = (
        device * col_share + lax.broadcasted_iota(jnp.int32, (KY, col_share), 1)
    ) // 2 - KZ // 2
    y_mode = lax.broadcasted_iota(jnp.int32, (KY, col_share), 0) - KY // 2
    wave_sq = (2.0 * jnp.sin(math.pi * y_mode.astype(jnp.float32) / NY)) ** 2 + (
        2.0 * jnp.sin(math.pi * z_mode.astype(jnp.float32) / NZ)
    ) ** 2
    is_zero = (y_mode == 0) & (z_mode == 0)
    scr = screen[:, None, None]
    green_fn = jnp.where(is_zero[None], jnp.zeros_like(wave_sq)[None], -scr / (wave_sq[None] + scr))
    return mode_values * green_fn * (1.0 / math.sqrt(NY * NZ))


def solution(mesh):
    return jax.shard_map(
        shards,
        mesh=mesh,
        in_specs=(
            P(("px", "py"), None),
            P(("px", "py"), None),
            P(("px", "py"), None),
            P(("px", "py")),
            P(),
        ),
        out_specs=P(None, None, ("px", "py")),
        check_vma=False,
    )
```

profile of v0, /device:TPU:1, one launch (start us, length us, event | category | flops | bytes accessed | tf_op | source)
XLA Modules:
  0.0 397.7 jit_solution(6626434158525641063)
XLA Ops:
  0.0 1.3 convert_reduce_fusion
  2.0 4.2 %scatter_custom_fusion.1 = bf16[2048,128]{1,0:T(8,128)(2,1)S(1)} fusion(s32[1024]{0:T(1024)S(1)} %bitcast.66, bf16[1024,128]{1,0:T(8,128)(2,1)} %param.8, s32[1024]{0:T(1024)} %param.10, bf16[]{:T(256)} %constant.186.clone.1), kind=kCustom, calls=%fused_computation.71 | custom fusion | flops 262144 | bytes 791552 | tf_op jit(solution)/shard_map/scatter | solution.py:58
  7.3 11.5 %all-to-all-start.1 = ((bf16[8,128,2,128]{3,2,0,1:T(2,128)(2,1)}), bf16[8,128,2,128]{3,2,0,1:T(2,128)(2,1)S(1)}, u32[]{:S(2)}, u32[]{:S(2)}) async-start(bf16[8,128,2,128]{3,2,0,1:T(2,128)(2,1)} %copy.31), calls=%async_computation.1 | async-start | bytes 1048576 | tf_op jit(solution)/shard_map/all_to_all | solution.py:64
  18.8 3.7 scatter_custom_fusion
  22.6 1.3 copy.29
  23.9 8.8 %all-to-all-done.1 = bf16[8,128,2,128]{3,2,0,1:T(2,128)(2,1)S(1)} async-done(((bf16[8,128,2,128]{3,2,0,1:T(2,128)(2,1)}), bf16[8,128,2,128]{3,2,0,1:T(2,128)(2,1)S(1)}, u32[]{:S(2)}, u32[]{:S(2)}) %all-to-all-start.1) | async-done | bytes 524320 | tf_op jit(solution)/shard_map/all_to_all | solution.py:64
  32.7 4.2 %all-to-all-start = ((s32[8,128,2,128]{3,2,0,1:T(2,128)}), s32[8,128,2,128]{3,2,0,1:T(2,128)S(1)}, u32[]{:S(2)}, u32[]{:S(2)}) async-start(s32[8,128,2,128]{3,2,0,1:T(2,128)} %copy.29), calls=%async_computation | async-start | bytes 2097152 | tf_op jit(solution)/shard_map/all_to_all | solution.py:63
  38.5 17.5 %all-to-all-done = s32[8,128,2,128]{3,2,0,1:T(2,128)S(1)} async-done(((s32[8,128,2,128]{3,2,0,1:T(2,128)}), s32[8,128,2,128]{3,2,0,1:T(2,128)S(1)}, u32[]{:S(2)}, u32[]{:S(2)}) %all-to-all-start) | async-done | bytes 1048608 | tf_op jit(solution)/shard_map/all_to_all | solution.py:63
  57.2 279.7 %while.12 = (s32[]{:T(128)}, f32[8,256,128]{2,0,1:T(8,128)}, s32[8,32768]{1,0:T(8,128)S(1)}, bf16[8,32768]{1,0:T(8,128)(2,1)}, s32[]{:T(128)}, /*index=5*/s32[]{:T(128)}) while((s32[]{:T(128)}, f32[8,256,128]{2,0,1:T(8,128)}, s32[8,32768]{1,0:T(8,128)S(1)}, bf16[8,32768]{1,0:T(8,128)(2,1)}, s32[]{:T(128)}, /*index=5*/s32[]{:T(128)}) %tuple.34), condition=%wide.region_4.5_spmd, body=%wide.region_3.4_spmd.sunk | while | flops 2164883456 | bytes 18284624 | solution.py:83
  57.9 1.5 dynamic-slice_reduce_fusion.2
  59.4 12.0 %fusion.88 = bf16[32768,128]{1,0:T(8,128)(2,1)} fusion(s32[32768]{0:T(1024)S(1)} %get-tuple-element.110, bf16[32768]{0:T(1024)(128)(2,1)S(1)} %dynamic-slice_reduce_fusion.2), kind=kLoop, calls=%fused_computation.6.clone.clone.2.clone.1 | loop fusion | flops 8388608 | bytes 8585216 | tf_op jit(solution)/shard_map/while/body/eval_jaxpr/dot_general | solution.py:79
  71.4 16.6 %fusion.89 = f32[256,128]{1,0:T(8,128)S(1)} fusion(s32[32768]{0:T(1024)S(1)} %get-tuple-element.109, bf16[32768,128]{1,0:T(8,128)(2,1)} %fusion.88), kind=kOutput, calls=%fused_computation.3.clone.3 | convolution fusion | flops 2155872256 | bytes 8650752 | tf_op jit(solution)/shard_map/while/body/eval_jaxpr/dot_general | solution.py:79
  87.9 4.7 %dynamic_update_slice.8 = f32[8,256,128]{2,0,1:T(8,128)} dynamic-update-slice(f32[8,256,128]{2,0,1:T(8,128)} %get-tuple-element.118, f32[1,256,128]{2,0,1:T(1,128)S(1)} %bitcast.63, s32[]{:T(128)} %get-tuple-element.117, s32[]{:T(128)} %constant.176.clone.1..sunk, s32[]{:T(128)} %constant.176.clone.1..sunk) | dynamic-update-slice | bytes 262148 | tf_op jit(solution)/shard_map/while/body/jit(dynamic_update_index_in_dim)/dynamic_update_slice | solution.py:83
  92.8 1.5 dynamic-slice_reduce_fusion.2
  94.3 12.0 %fusion.88 = bf16[32768,128]{1,0:T(8,128)(2,1)} fusion(s32[32768]{0:T(1024)S(1)} %get-tuple-element.110, bf16[32768]{0:T(1024)(128)(2,1)S(1)} %dynamic-slice_reduce_fusion.2), kind=kLoop, calls=%fused_computation.6.clone.clone.2.clone.1 | loop fusion | flops 8388608 | bytes 8585216 | tf_op jit(solution)/shard_map/while/body/eval_jaxpr/dot_general | solution.py:79
  106.3 16.6 %fusion.89 = f32[256,128]{1,0:T(8,128)S(1)} fusion(s32[32768]{0:T(1024)S(1)} %get-tuple-element.109, bf16[32768,128]{1,0:T(8,128)(2,1)} %fusion.88), kind=kOutput, calls=%fused_computation.3.clone.3 | convolution fusion | flops 2155872256 | bytes 8650752 | tf_op jit(solution)/shard_map/while/body/eval_jaxpr/dot_general | solution.py:79
  122.8 4.7 %dynamic_update_slice.8 = f32[8,256,128]{2,0,1:T(8,128)} dynamic-update-slice(f32[8,256,128]{2,0,1:T(8,128)} %get-tuple-element.118, f32[1,256,128]{2,0,1:T(1,128)S(1)} %bitcast.63, s32[]{:T(128)} %get-tuple-element.117, s32[]{:T(128)} %constant.176.clone.1..sunk, s32[]{:T(128)} %constant.176.clone.1..sunk) | dynamic-update-slice | bytes 262148 | tf_op jit(solution)/shard_map/while/body/jit(dynamic_update_index_in_dim)/dynamic_update_slice | solution.py:83
  127.7 1.5 dynamic-slice_reduce_fusion.2
  129.2 12.0 %fusion.88 = bf16[32768,128]{1,0:T(8,128)(2,1)} fusion(s32[32768]{0:T(1024)S(1)} %get-tuple-element.110, bf16[32768]{0:T(1024)(128)(2,1)S(1)} %dynamic-slice_reduce_fusion.2), kind=kLoop, calls=%fused_computation.6.clone.clone.2.clone.1 | loop fusion | flops 8388608 | bytes 8585216 | tf_op jit(solution)/shard_map/while/body/eval_jaxpr/dot_general | solution.py:79
  141.1 16.6 %fusion.89 = f32[256,128]{1,0:T(8,128)S(1)} fusion(s32[32768]{0:T(1024)S(1)} %get-tuple-element.109, bf16[32768,128]{1,0:T(8,128)(2,1)} %fusion.88), kind=kOutput, calls=%fused_computation.3.clone.3 | convolution fusion | flops 2155872256 | bytes 8650752 | tf_op jit(solution)/shard_map/while/body/eval_jaxpr/dot_general | solution.py:79
  157.7 4.7 %dynamic_update_slice.8 = f32[8,256,128]{2,0,1:T(8,128)} dynamic-update-slice(f32[8,256,128]{2,0,1:T(8,128)} %get-tuple-element.118, f32[1,256,128]{2,0,1:T(1,128)S(1)} %bitcast.63, s32[]{:T(128)} %get-tuple-element.117, s32[]{:T(128)} %constant.176.clone.1..sunk, s32[]{:T(128)} %constant.176.clone.1..sunk) | dynamic-update-slice | bytes 262148 | tf_op jit(solution)/shard_map/while/body/jit(dynamic_update_index_in_dim)/dynamic_update_slice | solution.py:83
  162.6 1.5 dynamic-slice_reduce_fusion.2
  164.0 12.0 %fusion.88 = bf16[32768,128]{1,0:T(8,128)(2,1)} fusion(s32[32768]{0:T(1024)S(1)} %get-tuple-element.110, bf16[32768]{0:T(1024)(128)(2,1)S(1)} %dynamic-slice_reduce_fusion.2), kind=kLoop, calls=%fused_computation.6.clone.clone.2.clone.1 | loop fusion | flops 8388608 | bytes 8585216 | tf_op jit(solution)/shard_map/while/body/eval_jaxpr/dot_general | solution.py:79
  176.0 16.6 %fusion.89 = f32[256,128]{1,0:T(8,128)S(1)} fusion(s32[32768]{0:T(1024)S(1)} %get-tuple-element.109, bf16[32768,128]{1,0:T(8,128)(2,1)} %fusion.88), kind=kOutput, calls=%fused_computation.3.clone.3 | convolution fusion | flops 2155872256 | bytes 8650752 | tf_op jit(solution)/shard_map/while/body/eval_jaxpr/dot_general | solution.py:79
  192.6 4.7 %dynamic_update_slice.8 = f32[8,256,128]{2,0,1:T(8,128)} dynamic-update-slice(f32[8,256,128]{2,0,1:T(8,128)} %get-tuple-element.118, f32[1,256,128]{2,0,1:T(1,128)S(1)} %bitcast.63, s32[]{:T(128)} %get-tuple-element.117, s32[]{:T(128)} %constant.176.clone.1..sunk, s32[]{:T(128)} %constant.176.clone.1..sunk) | dynamic-update-slice | bytes 262148 | tf_op jit(solution)/shard_map/while/body/jit(dynamic_update_index_in_dim)/dynamic_update_slice | solution.py:83
  197.5 1.5 dynamic-slice_reduce_fusion.2
  198.9 12.0 %fusion.88 = bf16[32768,128]{1,0:T(8,128)(2,1)} fusion(s32[32768]{0:T(1024)S(1)} %get-tuple-element.110, bf16[32768]{0:T(1024)(128)(2,1)S(1)} %dynamic-slice_reduce_fusion.2), kind=kLoop, calls=%fused_computation.6.clone.clone.2.clone.1 | loop fusion | flops 8388608 | bytes 8585216 | tf_op jit(solution)/shard_map/while/body/eval_jaxpr/dot_general | solution.py:79
  210.9 16.6 %fusion.89 = f32[256,128]{1,0:T(8,128)S(1)} fusion(s32[32768]{0:T(1024)S(1)} %get-tuple-element.109, bf16[32768,128]{1,0:T(8,128)(2,1)} %fusion.88), kind=kOutput, calls=%fused_computation.3.clone.3 | convolution fusion | flops 2155872256 | bytes 8650752 | tf_op jit(solution)/shard_map/while/body/eval_jaxpr/dot_general | solution.py:79
  227.4 4.7 %dynamic_update_slice.8 = f32[8,256,128]{2,0,1:T(8,128)} dynamic-update-slice(f32[8,256,128]{2,0,1:T(8,128)} %get-tuple-element.118, f32[1,256,128]{2,0,1:T(1,128)S(1)} %bitcast.63, s32[]{:T(128)} %get-tuple-element.117, s32[]{:T(128)} %constant.176.clone.1..sunk, s32[]{:T(128)} %constant.176.clone.1..sunk) | dynamic-update-slice | bytes 262148 | tf_op jit(solution)/shard_map/while/body/jit(dynamic_update_index_in_dim)/dynamic_update_slice | solution.py:83
  232.3 1.5 dynamic-slice_reduce_fusion.2
  233.8 12.0 %fusion.88 = bf16[32768,128]{1,0:T(8,128)(2,1)} fusion(s32[32768]{0:T(1024)S(1)} %get-tuple-element.110, bf16[32768]{0:T(1024)(128)(2,1)S(1)} %dynamic-slice_reduce_fusion.2), kind=kLoop, calls=%fused_computation.6.clone.clone.2.clone.1 | loop fusion | flops 8388608 | bytes 8585216 | tf_op jit(solution)/shard_map/while/body/eval_jaxpr/dot_general | solution.py:79
  245.8 16.6 %fusion.89 = f32[256,128]{1,0:T(8,128)S(1)} fusion(s32[32768]{0:T(1024)S(1)} %get-tuple-element.109, bf16[32768,128]{1,0:T(8,128)(2,1)} %fusion.88), kind=kOutput, calls=%fused_computation.3.clone.3 | convolution fusion | flops 2155872256 | bytes 8650752 | tf_op jit(solution)/shard_map/while/body/eval_jaxpr/dot_general | solution.py:79
  262.3 4.7 %dynamic_update_slice.8 = f32[8,256,128]{2,0,1:T(8,128)} dynamic-update-slice(f32[8,256,128]{2,0,1:T(8,128)} %get-tuple-element.118, f32[1,256,128]{2,0,1:T(1,128)S(1)} %bitcast.63, s32[]{:T(128)} %get-tuple-element.117, s32[]{:T(128)} %constant.176.clone.1..sunk, s32[]{:T(128)} %constant.176.clone.1..sunk) | dynamic-update-slice | bytes 262148 | tf_op jit(solution)/shard_map/while/body/jit(dynamic_update_index_in_dim)/dynamic_update_slice | solution.py:83
  267.2 1.5 dynamic-slice_reduce_fusion.2
  268.7 12.0 %fusion.88 = bf16[32768,128]{1,0:T(8,128)(2,1)} fusion(s32[32768]{0:T(1024)S(1)} %get-tuple-element.110, bf16[32768]{0:T(1024)(128)(2,1)S(1)} %dynamic-slice_reduce_fusion.2), kind=kLoop, calls=%fused_computation.6.clone.clone.2.clone.1 | loop fusion | flops 8388608 | bytes 8585216 | tf_op jit(solution)/shard_map/while/body/eval_jaxpr/dot_general | solution.py:79
  280.7 16.6 %fusion.89 = f32[256,128]{1,0:T(8,128)S(1)} fusion(s32[32768]{0:T(1024)S(1)} %get-tuple-element.109, bf16[32768,128]{1,0:T(8,128)(2,1)} %fusion.88), kind=kOutput, calls=%fused_computation.3.clone.3 | convolution fusion | flops 2155872256 | bytes 8650752 | tf_op jit(solution)/shard_map/while/body/eval_jaxpr/dot_general | solution.py:79
  297.2 4.7 %dynamic_update_slice.8 = f32[8,256,128]{2,0,1:T(8,128)} dynamic-update-slice(f32[8,256,128]{2,0,1:T(8,128)} %get-tuple-element.118, f32[1,256,128]{2,0,1:T(1,128)S(1)} %bitcast.63, s32[]{:T(128)} %get-tuple-element.117, s32[]{:T(128)} %constant.176.clone.1..sunk, s32[]{:T(128)} %constant.176.clone.1..sunk) | dynamic-update-slice | bytes 262148 | tf_op jit(solution)/shard_map/while/body/jit(dynamic_update_index_in_dim)/dynamic_update_slice | solution.py:83
  302.1 1.5 dynamic-slice_reduce_fusion.2
  303.6 12.0 %fusion.88 = bf16[32768,128]{1,0:T(8,128)(2,1)} fusion(s32[32768]{0:T(1024)S(1)} %get-tuple-element.110, bf16[32768]{0:T(1024)(128)(2,1)S(1)} %dynamic-slice_reduce_fusion.2), kind=kLoop, calls=%fused_computation.6.clone.clone.2.clone.1 | loop fusion | flops 8388608 | bytes 8585216 | tf_op jit(solution)/shard_map/while/body/eval_jaxpr/dot_general | solution.py:79
  315.5 16.6 %fusion.89 = f32[256,128]{1,0:T(8,128)S(1)} fusion(s32[32768]{0:T(1024)S(1)} %get-tuple-element.109, bf16[32768,128]{1,0:T(8,128)(2,1)} %fusion.88), kind=kOutput, calls=%fused_computation.3.clone.3 | convolution fusion | flops 2155872256 | bytes 8650752 | tf_op jit(solution)/shard_map/while/body/eval_jaxpr/dot_general | solution.py:79
  332.1 4.7 %dynamic_update_slice.8 = f32[8,256,128]{2,0,1:T(8,128)} dynamic-update-slice(f32[8,256,128]{2,0,1:T(8,128)} %get-tuple-element.118, f32[1,256,128]{2,0,1:T(1,128)S(1)} %bitcast.63, s32[]{:T(128)} %get-tuple-element.117, s32[]{:T(128)} %constant.176.clone.1..sunk, s32[]{:T(128)} %constant.176.clone.1..sunk) | dynamic-update-slice | bytes 262148 | tf_op jit(solution)/shard_map/while/body/jit(dynamic_update_index_in_dim)/dynamic_update_slice | solution.py:83
  336.9 3.7 all-to-all-start.2
  340.8 15.1 %all-to-all-done.2 = f32[8,256,128]{2,0,1:T(8,128)S(1)} async-done(((f32[8,256,128]{2,0,1:T(8,128)}), f32[8,256,128]{2,0,1:T(8,128)S(1)}, u32[]{:S(2)}, u32[]{:S(2)}) %all-to-all-start.2) | async-done | bytes 1048608 | tf_op jit(solution)/shard_map/all_to_all | solution.py:84
  356.7 9.5 %fusion.14 = f32[8,16,256]{2,1,0:T(8,128)S(1)} fusion(f32[8,16,2048]{2,1,0:T(8,128)S(1)} %dot_general.17, s32[256]{0:T(256)S(1)} %get-tuple-element.74, s32[256]{0:T(256)S(1)} %get-tuple-element.79, s32[256]{0:T(256)S(1)} %get-tuple-element.75, s32[256]{0:T(256)S(1)} %get-tuple-element.78, pred[256]{0:T(512)(128)(4,1)S(1)} %get-tuple-element.76, ...), kind=kOutput, calls=%fused_computation.30 | convolution fusion | flops 815792128 | bytes 1184256 | tf_op jit(solution)/shard_map/dot_general | solution.py:86
  367.7 6.7 %all-to-all-start.3 = ((f32[128,1,256]{2,1,0:T(1,128)}), f32[128,1,256]{2,1,0:T(1,128)S(1)}, u32[]{:S(2)}, u32[]{:S(2)}) async-start(f32[128,1,256]{2,1,0:T(1,128)} %reshape.223), calls=%async_computation.3 | async-start | bytes 262144 | tf_op jit(solution)/shard_map/all_to_all | solution.py:94
  374.5 10.0 %all-to-all-done.3 = f32[128,1,256]{2,1,0:T(1,128)S(1)} async-done(((f32[128,1,256]{2,1,0:T(1,128)}), f32[128,1,256]{2,1,0:T(1,128)S(1)}, u32[]{:S(2)}, u32[]{:S(2)}) %all-to-all-start.3) | async-done | bytes 131104 | tf_op jit(solution)/shard_map/all_to_all | solution.py:94
  387.4 4.7 %convolution_bitcast_fusion = f32[8,128,2]{1,0,2:T(8,128)S(1)} fusion(f32[8,2048,2]{1,0,2:T(8,128)S(1)} %all_to_all.38, s32[128]{0:T(128)S(1)} %iota_add_fusion.1), kind=kOutput, calls=%fused_computation.43 | convolution fusion | flops 54001664 | bytes 139776 | tf_op jit(solution)/shard_map/kp,lpc->lkc/dot_general | solution.py:27
  392.1 4.7 %convolution_bitcast_fusion.1 = f32[8,128,2]{1,0,2:T(8,128)S(1)} fusion(f32[8,2048,2]{1,0,2:T(8,128)S(1)} %all_to_all.38, s32[128]{0:T(128)S(1)} %iota_add_fusion.1), kind=kOutput, calls=%fused_computation.44 | convolution fusion | flops 54001664 | bytes 139776 | tf_op jit(solution)/shard_map/kp,lpc->lkc/dot_general | solution.py:26
  (48 shorter events, 12.3 us)
Async XLA Ops:
  7.3 25.4 %all-to-all-start.1 = ((bf16[8,128,2,128]{3,2,0,1:T(2,128)(2,1)}), bf16[8,128,2,128]{3,2,0,1:T(2,128)(2,1)S(1)}, u32[]{:S(2)}, u32[]{:S(2)}) async-start(bf16[8,128,2,128]{3,2,0,1:T(2,128)(2,1)} %copy.31), calls=%async_computation.1 | async-start | bytes 1048576 | tf_op jit(solution)/shard_map/all_to_all | solution.py:64
  32.7 23.3 %all-to-all-start = ((s32[8,128,2,128]{3,2,0,1:T(2,128)}), s32[8,128,2,128]{3,2,0,1:T(2,128)S(1)}, u32[]{:S(2)}, u32[]{:S(2)}) async-start(s32[8,128,2,128]{3,2,0,1:T(2,128)} %copy.29), calls=%async_computation | async-start | bytes 2097152 | tf_op jit(solution)/shard_map/all_to_all | solution.py:63
  336.9 19.0 %all-to-all-start.2 = ((f32[8,256,128]{2,0,1:T(8,128)}), f32[8,256,128]{2,0,1:T(8,128)S(1)}, u32[]{:S(2)}, u32[]{:S(2)}) async-start(f32[8,256,128]{2,0,1:T(8,128)} %get-tuple-element.61), calls=%async_computation.2 | async-start | bytes 2097152 | tf_op jit(solution)/shard_map/all_to_all | solution.py:84
  366.2 8.3 %copy-start = (f32[8]{0:T(128)S(1)}, f32[8]{0:T(128)}, u32[]{:S(2)}) copy-start(f32[8]{0:T(128)} %param.11) | copy-start | bytes 100
  367.7 16.9 %all-to-all-start.3 = ((f32[128,1,256]{2,1,0:T(1,128)}), f32[128,1,256]{2,1,0:T(1,128)S(1)}, u32[]{:S(2)}, u32[]{:S(2)}) async-start(f32[128,1,256]{2,1,0:T(1,128)} %reshape.223), calls=%async_computation.3 | async-start | bytes 262144 | tf_op jit(solution)/shard_map/all_to_all | solution.py:94
where the time goes:
time: 405 us; the launch traced here: 398 us
  matrix products  151 us (37%)
  other arithmetic  104 us (26%)
  local copies, waits for them, and re-layouts  63.4 us (16%)
  waiting for transfers between devices  51.4 us (13%)
  starting transfers between devices  26.1 us (6%)
    dot_general x8, matrix products, deposit(): lax.dot_general(onehot_rows, mass_cols, (((0,), (0,)), ((), ())), preferr...  132 us
    dot_general x8, other arithmetic, deposit(): lax.dot_general(onehot_rows, mass_cols, (((0,), (0,)), ((), ())), preferr...  95.8 us
    dynamic_update_slice x8, local copies, waits for them, and re-layouts, shards(): density = lax.map(deposit, (plane_cells, plane_mass))  37.4 us
    all_to_all x1, waiting for transfers between devices, shards(): lax.all_to_all(send_cells, ('px', 'py'), split_axis=1, concat_axis=1, til...  17.5 us
    all_to_all x1, waiting for transfers between devices, shards(): lax.all_to_all(density, 'py', split_axis=1, concat_axis=2, tiled=True)  15.1 us
    dynamic_slice x16, local copies, waits for them, and re-layouts, shards(): density = lax.map(deposit, (plane_cells, plane_mass))  12.4 us
    all_to_all x1, starting transfers between devices, shards(): lax.all_to_all(send_mass, ('px', 'py'), split_axis=1, concat_axis=1, tile...  11.5 us
    all_to_all x1, waiting for transfers between devices, shards(): lax.all_to_all(spectra, ('px', 'py'), split_axis=2, concat_axis=1, tiled=...  10 us
  transfers between devices with their start and end apart: 4, of which 4 were waited for; matrix products, arithmetic and copies ran while one was open for 2% of the time, Pallas kernels for 0%

commit v1 on v0

--- a/solution.py
+++ b/solution.py
@@ -81,7 +81,10 @@
         )
 
     density = lax.map(deposit, (plane_cells, plane_mass))
-    z_slab = lax.all_to_all(density, "py", split_axis=1, concat_axis=2, tiled=True)
+    z_slab = jnp.concatenate(
+        lax.all_to_all(jnp.stack(jnp.split(density, lax.axis_size("py"), axis=1)), "py", 0, 0),
+        axis=2,
+    )
     ztable = column_table(NZ)
     spectra = jnp.dot(
         z_slab.reshape(num_planes * row_share, NZ),

time: 405 us -> 387 us (0.956)
  local copies, waits for them, and re-layouts: 63.4 us -> 39.5 us
  matrix products: 151 us -> 157 us
    dynamic_update_slice x8 -> x0, local copies, waits for them, and re-layouts: 37.4 us -> none  [shards(): density = lax.map(deposit, (plane_cells, plane_mass))]
    unnamed x4 -> x19, local copies, waits for them, and re-layouts: 1.36 us -> 23.3 us
    dynamic_slice x16, local copies, waits for them, and re-layouts: 12.4 us -> 3.97 us  [shards(): density = lax.map(deposit, (plane_cells, plane_mass))]
    dot_general x8, matrix products: 132 us -> 138 us  [deposit(): lax.dot_general(onehot_rows, mass_cols, (((0,), (0,)), ((), ())), preferr...]
where the time goes in v1:
time: 387 us; the launch traced here: 380 us
  matrix products  157 us (41%)
  other arithmetic  104 us (27%)
  waiting for transfers between devices  52 us (13%)
  local copies, waits for them, and re-layouts  39.5 us (10%)
  starting transfers between devices  26.4 us (7%)
    dot_general x8, matrix products, deposit(): lax.dot_general(onehot_rows, mass_cols, (((0,), (0,)), ((), ())), preferr...  138 us
    dot_general x8, other arithmetic, deposit(): lax.dot_general(onehot_rows, mass_cols, (((0,), (0,)), ((), ())), preferr...  95.8 us
    unnamed x19, local copies, waits for them, and re-layouts  23.3 us
    all_to_all x1, waiting for transfers between devices, shards(): lax.all_to_all(send_cells, ('px', 'py'), split_axis=1, concat_axis=1, til...  18.3 us
    all_to_all x1, waiting for transfers between devices, shards(): lax.all_to_all(jnp.stack(jnp.split(density, lax.axis_size('py'), axis=1))...  15.1 us
    all_to_all x1, starting transfers between devices, shards(): lax.all_to_all(send_mass, ('px', 'py'), split_axis=1, concat_axis=1, tile...  11.5 us
    all_to_all x1, waiting for transfers between devices, shards(): lax.all_to_all(spectra, ('px', 'py'), split_axis=2, concat_axis=1, tiled=...  9.87 us
    dot_general x1, matrix products, shards(): jnp.dot(z_slab.reshape(num_planes * row_share, NZ), ztable, precision=HIG...  9.55 us
  transfers between devices with their start and end apart: 4, of which 4 were waited for; matrix products, arithmetic and copies ran while one was open for 2% of the time, Pallas kernels for 0%

profile of v1, /device:TPU:1, one launch (start us, length us, event | category | flops | bytes accessed | tf_op | source)
XLA Modules:
  0.0 379.9 jit_solution(12098528041521756518)
XLA Ops:
  0.0 1.3 convert_reduce_fusion
  2.0 4.2 %scatter_custom_fusion.1 = bf16[2048,128]{1,0:T(8,128)(2,1)S(1)} fusion(s32[1024]{0:T(1024)S(1)} %bitcast.99, bf16[1024,128]{1,0:T(8,128)(2,1)} %param.8, s32[1024]{0:T(1024)} %param.10, bf16[]{:T(256)} %constant.186.clone.1), kind=kCustom, calls=%fused_computation.74 | custom fusion | flops 262144 | bytes 791552 | tf_op jit(solution)/shard_map/scatter | solution.py:58
  7.3 11.5 %all-to-all-start.1 = ((bf16[8,128,2,128]{3,2,0,1:T(2,128)(2,1)}), bf16[8,128,2,128]{3,2,0,1:T(2,128)(2,1)S(1)}, u32[]{:S(2)}, u32[]{:S(2)}) async-start(bf16[8,128,2,128]{3,2,0,1:T(2,128)(2,1)} %copy.29), calls=%async_computation.1 | async-start | bytes 1048576 | tf_op jit(solution)/shard_map/all_to_all | solution.py:64
  18.8 3.7 scatter_custom_fusion
  22.6 1.3 copy.27
  23.9 8.8 %all-to-all-done.1 = bf16[8,128,2,128]{3,2,0,1:T(2,128)(2,1)S(1)} async-done(((bf16[8,128,2,128]{3,2,0,1:T(2,128)(2,1)}), bf16[8,128,2,128]{3,2,0,1:T(2,128)(2,1)S(1)}, u32[]{:S(2)}, u32[]{:S(2)}) %all-to-all-start.1) | async-done | bytes 524320 | tf_op jit(solution)/shard_map/all_to_all | solution.py:64
  32.7 4.2 %all-to-all-start = ((s32[8,128,2,128]{3,2,0,1:T(2,128)}), s32[8,128,2,128]{3,2,0,1:T(2,128)S(1)}, u32[]{:S(2)}, u32[]{:S(2)}) async-start(s32[8,128,2,128]{3,2,0,1:T(2,128)} %copy.27), calls=%async_computation | async-start | bytes 2097152 | tf_op jit(solution)/shard_map/all_to_all | solution.py:63
  37.7 18.3 %all-to-all-done = s32[8,128,2,128]{3,2,0,1:T(2,128)S(1)} async-done(((s32[8,128,2,128]{3,2,0,1:T(2,128)}), s32[8,128,2,128]{3,2,0,1:T(2,128)S(1)}, u32[]{:S(2)}, u32[]{:S(2)}) %all-to-all-start) | async-done | bytes 1048608 | tf_op jit(solution)/shard_map/all_to_all | solution.py:63
  57.2 239.1 %while.12 = (s32[]{:T(128)}, f32[8,256,128]{2,1,0:T(8,128)}, s32[8,32768]{1,0:T(8,128)S(1)}, bf16[8,32768]{1,0:T(8,128)(2,1)S(1)}, s32[]{:T(128)}) while((s32[]{:T(128)}, f32[8,256,128]{2,1,0:T(8,128)}, s32[8,32768]{1,0:T(8,128)S(1)}, bf16[8,32768]{1,0:T(8,128)(2,1)S(1)}, s32[]{:T(128)}) %tuple.34), condition=%wide.region_4.5_spmd, body=%wide.region_3.4_spmd.sunk | while | flops 2164883456 | bytes 18022980 | solution.py:83
  58.3 12.0 %fusion.96 = bf16[32768,128]{1,0:T(8,128)(2,1)} fusion(s32[32768]{0:T(1024)S(1)} %get-tuple-element.110, bf16[32768]{0:T(1024)(128)(2,1)S(1)} %dynamic-slice_reduce_fusion.2), kind=kLoop, calls=%fused_computation.6.clone.clone.clone.clone.clone.clone.2.clone.1 | loop fusion | flops 8388608 | bytes 8585216 | tf_op jit(solution)/shard_map/while/body/eval_jaxpr/dot_general | solution.py:79
  70.3 17.2 %fusion.97 = f32[8,256,128]{2,1,0:T(8,128)} fusion(f32[8,256,128]{2,1,0:T(8,128)} %get-tuple-element.117, s32[]{:T(128)} %get-tuple-element.116, s32[32768]{0:T(1024)S(1)} %get-tuple-element.109, bf16[32768,128]{1,0:T(8,128)(2,1)} %fusion.96), kind=kOutput, calls=%fused_computation.11.clone.3 | convolution fusion | flops 2155872256 | bytes 8651264 | tf_op jit(solution)/shard_map/while/body/eval_jaxpr/dot_general | solution.py:79
  88.2 12.0 %fusion.96 = bf16[32768,128]{1,0:T(8,128)(2,1)} fusion(s32[32768]{0:T(1024)S(1)} %get-tuple-element.110, bf16[32768]{0:T(1024)(128)(2,1)S(1)} %dynamic-slice_reduce_fusion.2), kind=kLoop, calls=%fused_computation.6.clone.clone.clone.clone.clone.clone.2.clone.1 | loop fusion | flops 8388608 | bytes 8585216 | tf_op jit(solution)/shard_map/while/body/eval_jaxpr/dot_general | solution.py:79
  100.1 17.2 %fusion.97 = f32[8,256,128]{2,1,0:T(8,128)} fusion(f32[8,256,128]{2,1,0:T(8,128)} %get-tuple-element.117, s32[]{:T(128)} %get-tuple-element.116, s32[32768]{0:T(1024)S(1)} %get-tuple-element.109, bf16[32768,128]{1,0:T(8,128)(2,1)} %fusion.96), kind=kOutput, calls=%fused_computation.11.clone.3 | convolution fusion | flops 2155872256 | bytes 8651264 | tf_op jit(solution)/shard_map/while/body/eval_jaxpr/dot_general | solution.py:79
  118.0 12.0 %fusion.96 = bf16[32768,128]{1,0:T(8,128)(2,1)} fusion(s32[32768]{0:T(1024)S(1)} %get-tuple-element.110, bf16[32768]{0:T(1024)(128)(2,1)S(1)} %dynamic-slice_reduce_fusion.2), kind=kLoop, calls=%fused_computation.6.clone.clone.clone.clone.clone.clone.2.clone.1 | loop fusion | flops 8388608 | bytes 8585216 | tf_op jit(solution)/shard_map/while/body/eval_jaxpr/dot_general | solution.py:79
  130.0 17.2 %fusion.97 = f32[8,256,128]{2,1,0:T(8,128)} fusion(f32[8,256,128]{2,1,0:T(8,128)} %get-tuple-element.117, s32[]{:T(128)} %get-tuple-element.116, s32[32768]{0:T(1024)S(1)} %get-tuple-element.109, bf16[32768,128]{1,0:T(8,128)(2,1)} %fusion.96), kind=kOutput, calls=%fused_computation.11.clone.3 | convolution fusion | flops 2155872256 | bytes 8651264 | tf_op jit(solution)/shard_map/while/body/eval_jaxpr/dot_general | solution.py:79
  147.8 12.0 %fusion.96 = bf16[32768,128]{1,0:T(8,128)(2,1)} fusion(s32[32768]{0:T(1024)S(1)} %get-tuple-element.110, bf16[32768]{0:T(1024)(128)(2,1)S(1)} %dynamic-slice_reduce_fusion.2), kind=kLoop, calls=%fused_computation.6.clone.clone.clone.clone.clone.clone.2.clone.1 | loop fusion | flops 8388608 | bytes 8585216 | tf_op jit(solution)/shard_map/while/body/eval_jaxpr/dot_general | solution.py:79
  159.8 17.2 %fusion.97 = f32[8,256,128]{2,1,0:T(8,128)} fusion(f32[8,256,128]{2,1,0:T(8,128)} %get-tuple-element.117, s32[]{:T(128)} %get-tuple-element.116, s32[32768]{0:T(1024)S(1)} %get-tuple-element.109, bf16[32768,128]{1,0:T(8,128)(2,1)} %fusion.96), kind=kOutput, calls=%fused_computation.11.clone.3 | convolution fusion | flops 2155872256 | bytes 8651264 | tf_op jit(solution)/shard_map/while/body/eval_jaxpr/dot_general | solution.py:79
  177.6 12.0 %fusion.96 = bf16[32768,128]{1,0:T(8,128)(2,1)} fusion(s32[32768]{0:T(1024)S(1)} %get-tuple-element.110, bf16[32768]{0:T(1024)(128)(2,1)S(1)} %dynamic-slice_reduce_fusion.2), kind=kLoop, calls=%fused_computation.6.clone.clone.clone.clone.clone.clone.2.clone.1 | loop fusion | flops 8388608 | bytes 8585216 | tf_op jit(solution)/shard_map/while/body/eval_jaxpr/dot_general | solution.py:79
  189.6 17.2 %fusion.97 = f32[8,256,128]{2,1,0:T(8,128)} fusion(f32[8,256,128]{2,1,0:T(8,128)} %get-tuple-element.117, s32[]{:T(128)} %get-tuple-element.116, s32[32768]{0:T(1024)S(1)} %get-tuple-element.109, bf16[32768,128]{1,0:T(8,128)(2,1)} %fusion.96), kind=kOutput, calls=%fused_computation.11.clone.3 | convolution fusion | flops 2155872256 | bytes 8651264 | tf_op jit(solution)/shard_map/while/body/eval_jaxpr/dot_general | solution.py:79
  207.4 12.0 %fusion.96 = bf16[32768,128]{1,0:T(8,128)(2,1)} fusion(s32[32768]{0:T(1024)S(1)} %get-tuple-element.110, bf16[32768]{0:T(1024)(128)(2,1)S(1)} %dynamic-slice_reduce_fusion.2), kind=kLoop, calls=%fused_computation.6.clone.clone.clone.clone.clone.clone.2.clone.1 | loop fusion | flops 8388608 | bytes 8585216 | tf_op jit(solution)/shard_map/while/body/eval_jaxpr/dot_general | solution.py:79
  219.4 17.2 %fusion.97 = f32[8,256,128]{2,1,0:T(8,128)} fusion(f32[8,256,128]{2,1,0:T(8,128)} %get-tuple-element.117, s32[]{:T(128)} %get-tuple-element.116, s32[32768]{0:T(1024)S(1)} %get-tuple-element.109, bf16[32768,128]{1,0:T(8,128)(2,1)} %fusion.96), kind=kOutput, calls=%fused_computation.11.clone.3 | convolution fusion | flops 2155872256 | bytes 8651264 | tf_op jit(solution)/shard_map/while/body/eval_jaxpr/dot_general | solution.py:79
  237.2 12.0 %fusion.96 = bf16[32768,128]{1,0:T(8,128)(2,1)} fusion(s32[32768]{0:T(1024)S(1)} %get-tuple-element.110, bf16[32768]{0:T(1024)(128)(2,1)S(1)} %dynamic-slice_reduce_fusion.2), kind=kLoop, calls=%fused_computation.6.clone.clone.clone.clone.clone.clone.2.clone.1 | loop fusion | flops 8388608 | bytes 8585216 | tf_op jit(solution)/shard_map/while/body/eval_jaxpr/dot_general | solution.py:79
  249.2 17.2 %fusion.97 = f32[8,256,128]{2,1,0:T(8,128)} fusion(f32[8,256,128]{2,1,0:T(8,128)} %get-tuple-element.117, s32[]{:T(128)} %get-tuple-element.116, s32[32768]{0:T(1024)S(1)} %get-tuple-element.109, bf16[32768,128]{1,0:T(8,128)(2,1)} %fusion.96), kind=kOutput, calls=%fused_computation.11.clone.3 | convolution fusion | flops 2155872256 | bytes 8651264 | tf_op jit(solution)/shard_map/while/body/eval_jaxpr/dot_general | solution.py:79
  267.0 12.0 %fusion.96 = bf16[32768,128]{1,0:T(8,128)(2,1)} fusion(s32[32768]{0:T(1024)S(1)} %get-tuple-element.110, bf16[32768]{0:T(1024)(128)(2,1)S(1)} %dynamic-slice_reduce_fusion.2), kind=kLoop, calls=%fused_computation.6.clone.clone.clone.clone.clone.clone.2.clone.1 | loop fusion | flops 8388608 | bytes 8585216 | tf_op jit(solution)/shard_map/while/body/eval_jaxpr/dot_general | solution.py:79
  279.0 17.2 %fusion.97 = f32[8,256,128]{2,1,0:T(8,128)} fusion(f32[8,256,128]{2,1,0:T(8,128)} %get-tuple-element.117, s32[]{:T(128)} %get-tuple-element.116, s32[32768]{0:T(1024)S(1)} %get-tuple-element.109, bf16[32768,128]{1,0:T(8,128)(2,1)} %fusion.96), kind=kOutput, calls=%fused_computation.11.clone.3 | convolution fusion | flops 2155872256 | bytes 8651264 | tf_op jit(solution)/shard_map/while/body/eval_jaxpr/dot_general | solution.py:79
  296.4 1.5 bitcast_dynamic-update-slice_fusion.15
  297.8 1.5 bitcast_dynamic-update-slice_fusion.14
  299.3 1.5 bitcast_dynamic-update-slice_fusion.13
  300.8 1.5 bitcast_dynamic-update-slice_fusion.12
  302.2 1.5 bitcast_dynamic-update-slice_fusion.11
  303.7 1.5 bitcast_dynamic-update-slice_fusion.10
  305.2 1.5 bitcast_dynamic-update-slice_fusion.9
  306.6 1.5 bitcast_dynamic-update-slice_fusion.8
  308.1 1.5 bitcast_dynamic-update-slice_fusion.7
  309.5 1.5 bitcast_dynamic-update-slice_fusion.6
  311.0 1.5 bitcast_dynamic-update-slice_fusion.5
  312.5 1.5 bitcast_dynamic-update-slice_fusion.4
  313.9 1.5 bitcast_dynamic-update-slice_fusion.3
  315.4 1.5 bitcast_dynamic-update-slice_fusion.2
  316.9 1.5 bitcast_dynamic-update-slice_fusion.1
  318.3 1.5 bitcast_dynamic-update-slice_fusion
  319.8 3.7 all-to-all-start.2
  323.7 15.1 %all-to-all-done.2 = f32[16,8,16,128]{3,2,1,0:T(8,128)S(1)} async-done(((f32[16,8,16,128]{3,2,1,0:T(8,128)}), f32[16,8,16,128]{3,2,1,0:T(8,128)S(1)}, u32[]{:S(2)}, u32[]{:S(2)}) %all-to-all-start.2) | async-done | bytes 1048608 | tf_op jit(solution)/shard_map/all_to_all | solution.py:85
  338.8 9.5 %fusion.20 = f32[8,16,256]{2,1,0:T(8,128)S(1)} fusion(s32[256]{0:T(256)S(1)} %get-tuple-element.74, s32[256]{0:T(256)S(1)} %get-tuple-element.79, s32[256]{0:T(256)S(1)} %get-tuple-element.75, s32[256]{0:T(256)S(1)} %get-tuple-element.78, pred[256]{0:T(512)(128)(4,1)S(1)} %get-tuple-element.76, pred[256]{0:T(512)(128)(4,1)S(1)} %get-tuple-element.77, ...), kind=kOutput, calls=%fused_computation.32 | convolution fusion | flops 815792128 | bytes 1184256 | tf_op jit(solution)/shard_map/dot_general | solution.py:89
  349.8 7.0 %all-to-all-start.3 = ((f32[128,1,256]{2,1,0:T(1,128)}), f32[128,1,256]{2,1,0:T(1,128)S(1)}, u32[]{:S(2)}, u32[]{:S(2)}) async-start(f32[128,1,256]{2,1,0:T(1,128)} %reshape.225), calls=%async_computation.3 | async-start | bytes 262144 | tf_op jit(solution)/shard_map/all_to_all | solution.py:97
  356.9 9.9 %all-to-all-done.3 = f32[128,1,256]{2,1,0:T(1,128)S(1)} async-done(((f32[128,1,256]{2,1,0:T(1,128)}), f32[128,1,256]{2,1,0:T(1,128)S(1)}, u32[]{:S(2)}, u32[]{:S(2)}) %all-to-all-start.3) | async-done | bytes 131104 | tf_op jit(solution)/shard_map/all_to_all | solution.py:97
  369.6 4.7 %convolution_bitcast_fusion = f32[8,128,2]{1,0,2:T(8,128)S(1)} fusion(f32[8,2048,2]{1,0,2:T(8,128)S(1)} %all_to_all.28, s32[128]{0:T(128)S(1)} %iota_add_fusion.1), kind=kOutput, calls=%fused_computation.45 | convolution fusion | flops 54001664 | bytes 139776 | tf_op jit(solution)/shard_map/kp,lpc->lkc/dot_general | solution.py:27
  374.3 4.7 %convolution_bitcast_fusion.1 = f32[8,128,2]{1,0,2:T(8,128)S(1)} fusion(f32[8,2048,2]{1,0,2:T(8,128)S(1)} %all_to_all.28, s32[128]{0:T(128)S(1)} %iota_add_fusion.1), kind=kOutput, calls=%fused_computation.46 | convolution fusion | flops 54001664 | bytes 139776 | tf_op jit(solution)/shard_map/kp,lpc->lkc/dot_general | solution.py:26
  (54 shorter events, 14.0 us)
Async XLA Ops:
  7.3 25.4 %all-to-all-start.1 = ((bf16[8,128,2,128]{3,2,0,1:T(2,128)(2,1)}), bf16[8,128,2,128]{3,2,0,1:T(2,128)(2,1)S(1)}, u32[]{:S(2)}, u32[]{:S(2)}) async-start(bf16[8,128,2,128]{3,2,0,1:T(2,128)(2,1)} %copy.29), calls=%async_computation.1 | async-start | bytes 1048576 | tf_op jit(solution)/shard_map/all_to_all | solution.py:64
  32.7 23.3 %all-to-all-start = ((s32[8,128,2,128]{3,2,0,1:T(2,128)}), s32[8,128,2,128]{3,2,0,1:T(2,128)S(1)}, u32[]{:S(2)}, u32[]{:S(2)}) async-start(s32[8,128,2,128]{3,2,0,1:T(2,128)} %copy.27), calls=%async_computation | async-start | bytes 2097152 | tf_op jit(solution)/shard_map/all_to_all | solution.py:63
  319.8 19.0 %all-to-all-start.2 = ((f32[16,8,16,128]{3,2,1,0:T(8,128)}), f32[16,8,16,128]{3,2,1,0:T(8,128)S(1)}, u32[]{:S(2)}, u32[]{:S(2)}) async-start(f32[16,8,16,128]{3,2,1,0:T(8,128)} %bitcast_dynamic-update-slice_fusion), calls=%async_computation.2 | async-start | bytes 2097152 | tf_op jit(solution)/shard_map/all_to_all | solution.py:85
  348.3 8.6 %copy-start = (f32[8]{0:T(128)S(1)}, f32[8]{0:T(128)}, u32[]{:S(2)}) copy-start(f32[8]{0:T(128)} %param.11) | copy-start | bytes 100
  349.8 17.0 %all-to-all-start.3 = ((f32[128,1,256]{2,1,0:T(1,128)}), f32[128,1,256]{2,1,0:T(1,128)S(1)}, u32[]{:S(2)}, u32[]{:S(2)}) async-start(f32[128,1,256]{2,1,0:T(1,128)} %reshape.225), calls=%async_computation.3 | async-start | bytes 262144 | tf_op jit(solution)/shard_map/all_to_all | solution.py:97
